TPU v7x, 32 devices: a whole 2x2x4 slice. The times are simulated.
32 devices in a mesh: flow: 8 (over y, x, core), grad: 4 (over z).
Axes of the slice: x: 2, y: 2, z: 4, core: 2. Of those that a mesh axis runs over, the one named last changes fastest.
Arguments:
- positions: float32 [3, 4, 2048], P(None, 'grad', 'flow'), may hold values from 0 to 1
- features: float32 [4, 128, 2048], P('grad', None, 'flow'), may hold values from -6 to 6
- neighbours: int32 [4, 32, 2048], P('grad', None, 'flow'), may hold values from 0 to 1279, as said below
- face_blocks: int32 [4, 4, 16], P('grad', None, 'flow'), may hold values from 0 to 1
- shear_cells: int32 [1], replicated, may hold values from 0 to 7
- split_block: int32 [1], replicated, may hold values from 0 to 2
- radial_in: float32 [8, 64], replicated, may hold values from -2 to 2
- radial_out: float32 [64, 128], replicated, may hold values from -0.75 to 0.75
- mixing: float32 [3, 128, 128], replicated, may hold values from -0.3125 to 0.3125
- readout: float32 [128], replicated, may hold values from -0.5 to 0.5
Outputs:
- atom_energy: float32 [4, 2048], P('grad', 'flow')
- forces: float32 [3, 4, 2048], P(None, 'grad', 'flow')
Inputs may be any that keep to these rules, and one draw needn't show every extreme that they name: `neighbours`: each atom's 32 entries index its cell's extended list: the 256 own atoms, then 2 * 128 ghost atoms from each of the flow-lower, flow-upper, grad-lower and grad-upper sides, in that order. An atom never lists itself; entries may repeat. `face_blocks`: row k of a cell lists blocks of its own atoms that it shares: face 0 with the flow-upper cell, 1 with the flow-lower, 2 with the grad-upper, 3 with the grad-lower. Entries may repeat.
All inputs are finite; a program needn't handle non-finite values.
Results may differ from a plain program's by a relative error of at most 0.0003.
Values sent between devices are 32-bit elements; how exact they have to be, the bound alone decides.
No kernel may reach another device: no remote copies, remote signals or barrier semaphores. Data moves between devices by JAX's collectives and lax.ppermute only.
A program may use at most 64 MiB of HBM per device.

v0:
```python
import jax
import jax.numpy as jnp
from jax import lax
from jax.sharding import PartitionSpec as P

BLOCK = 128


highest = lax.Precision.HIGHEST
root_three = 3.0**0.5
root_five = 5.0**0.5
root_fifteen = 15.0**0.5


def from_behind(x, axis, by):
    peers = lax.axis_size(axis)
    return lax.ppermute(x, axis, [(i, (i + by) % peers) for i in range(peers)])


def harmonics(separation):
    xcoord = separation[0]
    ycoord = separation[1]
    zcoord = separation[2]
    square = xcoord * xcoord + ycoord * ycoord + zcoord * zcoord
    values = [
        jnp.ones_like(xcoord),
        root_three * xcoord,
        root_three * ycoord,
        root_three * zcoord,
        root_fifteen * xcoord * ycoord,
        root_fifteen * ycoord * zcoord,
        0.5 * root_five * (3.0 * zcoord * zcoord - square),
        root_fifteen * xcoord * zcoord,
        0.5 * root_fifteen * (xcoord * xcoord - ycoord * ycoord),
    ]
    return (jnp.stack(values), square)


def contribution(centre, group_pos, gathered, radial_in, radial_out):
    separation = group_pos - centre[:, None, :]
    harmonic, square = harmonics(separation)
    number = radial_in.shape[0]
    centres = jnp.arange(number, dtype=jnp.int32).astype(jnp.float32) * (6.0 / (number - 1))
    gaussians = jnp.exp(-0.5 * jnp.square((square[None] - centres[:, None, None]) / 0.75))
    hidden = jax.nn.silu(jnp.einsum("rh,rgb->hgb", radial_in, gaussians, precision=highest))
    radial = jnp.einsum("hc,hgb->gbc", radial_out, hidden, precision=highest)
    weighted = radial * gathered
    return jnp.einsum("gbc,mgb->mcb", weighted, harmonic, precision=highest)


def readout_energy(moments, mixing, readout):
    squared = moments * moments
    invariants = jnp.stack(
        [squared[0], squared[1] + squared[2] + squared[3], jnp.sum(squared[4:], axis=0)]
    )
    mixed = jnp.einsum("lcd,lcb->db", mixing, invariants, precision=highest)
    return jnp.einsum("d,db->b", readout, jax.nn.silu(mixed), precision=highest)


def one_hot_of(group_idx, extent):
    columns = jnp.arange(extent, dtype=jnp.int32)
    return (group_idx[:, :, None] == columns[None, None, :]).astype(jnp.float32)


def block_pass(centre, chosen, ext_pos, feat_rows, radial_in, radial_out, mixing, readout):
    neigh_count = chosen.shape[0]
    width = chosen.shape[1]
    extent = ext_pos.shape[1]
    channels = feat_rows.shape[1]
    grouping = 8
    rounds = neigh_count // grouping
    chosen_groups = chosen.reshape(rounds, grouping, width)
    factor = neigh_count ** (-0.5)

    def forward(running, group_idx):
        selector = one_hot_of(group_idx, extent)
        group_pos = jnp.einsum("pe,gbe->pgb", ext_pos, selector, precision=highest)
        gathered = jnp.take(feat_rows, group_idx.reshape(-1), axis=0).reshape(
            grouping, width, channels
        )
        running = running + contribution(centre, group_pos, gathered, radial_in, radial_out)
        return (running, (group_pos, gathered))

    starting = jnp.zeros((9, channels, width), jnp.float32)
    summed, (pos_groups, feat_groups) = lax.scan(forward, starting, chosen_groups)
    moments = summed * factor

    def head(moments_value):
        return readout_energy(moments_value, mixing, readout)

    energy, pullback = jax.vjp(head, moments)
    (cotangent,) = pullback(jnp.ones_like(energy))
    cotangent = cotangent * factor

    def backward(carry, pieces):
        grad_centre, grad_ext = carry
        group_pos, gathered, group_idx = pieces

        def local(centre_value, group_value):
            return contribution(centre_value, group_value, gathered, radial_in, radial_out)

        _, pullback_group = jax.vjp(local, centre, group_pos)
        centre_grad, group_grad = pullback_group(cotangent)
        selector = one_hot_of(group_idx, extent)
        grad_ext = grad_ext + jnp.einsum("pgb,gbe->pe", group_grad, selector, precision=highest)
        return ((grad_centre + centre_grad, grad_ext), None)

    start_carry = (jnp.zeros_like(centre), jnp.zeros(ext_pos.shape, jnp.float32))
    (grad_centre, grad_ext), _ = lax.scan(
        backward, start_carry, (pos_groups, feat_groups, chosen_groups)
    )
    return (energy, grad_centre, grad_ext)


def device_pass(ext_pos, features_all, neigh, radial_in, radial_out, mixing, readout, block):
    atom_count = neigh.shape[1]
    number = atom_count // block
    feat_rows = jnp.transpose(features_all)

    def step(gradient, step_index):
        anchor = step_index * block
        chosen = lax.dynamic_slice_in_dim(neigh, anchor, block, 1)
        centre = lax.dynamic_slice_in_dim(ext_pos, anchor, block, 1)
        energy, grad_centre, grad_ext = block_pass(
            centre, chosen, ext_pos, feat_rows, radial_in, radial_out, mixing, readout
        )
        gradient = gradient + grad_ext
        current = lax.dynamic_slice_in_dim(gradient, anchor, block, 1)
        gradient = lax.dynamic_update_slice_in_dim(gradient, current + grad_centre, anchor, 1)
        return (gradient, energy)

    gradient, energies = lax.scan(
        step, jnp.zeros(ext_pos.shape, jnp.float32), jnp.arange(number, dtype=jnp.int32)
    )
    return (energies.reshape(-1), gradient)


def flow_pass(payload, offset_by):
    return from_behind(payload, "flow", offset_by)


def grad_pass(payload, offset_by):
    return from_behind(payload, "grad", offset_by)


def step_shift(payload, offset_by):
    return from_behind(payload, "flow", offset_by)


def back_shift(payload, offset_by):
    return from_behind(payload, "flow", offset_by)


def flow_back(payload, offset_by):
    return from_behind(payload, "flow", offset_by)


def grad_back(payload, offset_by):
    return from_behind(payload, "grad", offset_by)


def doubled_route(payload, amount, direction, mover):
    levels = (lax.axis_size("flow") - 1).bit_length()
    for level in range(levels):
        moved = mover(payload, direction * (1 << level))
        flagged = jnp.bitwise_and(jnp.right_shift(amount, level), 1) == 1
        payload = jnp.where(flagged, moved, payload)
    return payload


def shear_offsets(ghost, sign, split):
    slots = jnp.arange(ghost, dtype=jnp.int32)[None, :, None]
    fraction = split.astype(jnp.float32) / ghost
    if sign > 0:
        return jnp.where(slots < split, fraction - 1.0, fraction)
    return jnp.where(slots < ghost - split, -fraction, 1.0 - fraction)


def sheared_in(payload, sign, offset, split):
    ghost = payload.shape[1]
    first = doubled_route(payload, offset, sign, step_shift)
    second = step_shift(first, sign)
    slots = jnp.arange(ghost, dtype=jnp.int32)[None, :, None]
    if sign > 0:
        early = slots < split
        return jnp.where(early, jnp.roll(second, split, axis=1), jnp.roll(first, split, axis=1))
    early = slots < ghost - split
    return jnp.where(early, jnp.roll(first, -split, axis=1), jnp.roll(second, -split, axis=1))


def sheared_out(gradient, sign, offset, split):
    ghost = gradient.shape[1]
    slots = jnp.arange(ghost, dtype=jnp.int32)[None, :, None]
    if sign > 0:
        keeping = slots >= split
        rolled_by = -split
    else:
        keeping = slots < ghost - split
        rolled_by = split
    nearer = jnp.roll(jnp.where(keeping, gradient, 0.0), rolled_by, axis=1)
    farther = jnp.roll(jnp.where(keeping, 0.0, gradient), rolled_by, axis=1)
    joined = nearer + back_shift(farther, -sign)
    return doubled_route(joined, offset, -sign, back_shift)


def block_selector(listed, count):
    return (listed[:, None] == jnp.arange(count, dtype=jnp.int32)[None, :]).astype(jnp.float32)


def body(
    positions,
    features,
    neighbours,
    face_blocks,
    shear_cells,
    split_block,
    radial_in,
    radial_out,
    mixing,
    readout,
):
    own_pos = positions[:, 0, :]
    own_feat = features[0]
    neigh = neighbours[0]
    faces = face_blocks[0]
    atom_count = own_pos.shape[1]
    ghost = faces.shape[1]
    channels = own_feat.shape[0]
    block_count = atom_count // BLOCK
    tiles = jnp.concatenate([own_pos, own_feat], axis=0).reshape(channels + 3, block_count, BLOCK)

    def picked(number):
        return jnp.einsum(
            "kn,cnt->ckt", block_selector(faces[number], block_count), tiles, precision=highest
        )

    row = lax.axis_index("grad")
    rows = lax.axis_size("grad")
    offset = shear_cells[0]
    split = split_block[0]
    low_wrap = row == 0
    high_wrap = row == rows - 1
    left = flow_pass(picked(0), 1)
    right = flow_pass(picked(1), -1)
    low_source = picked(2)
    high_source = picked(3)
    lower_plain = grad_pass(low_source, 1)
    upper_plain = grad_pass(high_source, -1)
    lower = jnp.where(low_wrap, sheared_in(lower_plain, 1, offset, split), lower_plain)
    upper = jnp.where(high_wrap, sheared_in(upper_plain, -1, offset, split), upper_plain)
    lower_x = jnp.where(low_wrap, shear_offsets(ghost, 1, split), 0.0)
    upper_x = jnp.where(high_wrap, shear_offsets(ghost, -1, split), 0.0)
    blank = jnp.zeros((1, ghost, BLOCK), jnp.float32)

    def placed(tile, xshift, yshift):
        shifts = jnp.concatenate([blank + xshift, blank + yshift, blank], axis=0)
        return ((tile[:3] + shifts).reshape(3, -1), tile[3:].reshape(channels, -1))

    groups = [
        placed(left, -1.0, 0.0),
        placed(right, 1.0, 0.0),
        placed(lower, lower_x, -1.0),
        placed(upper, upper_x, 1.0),
    ]
    ext_pos = jnp.concatenate([own_pos] + [entry[0] for entry in groups], axis=1)
    features_all = jnp.concatenate([own_feat] + [entry[1] for entry in groups], axis=1)
    energies, gradient = device_pass(
        ext_pos, features_all, neigh, radial_in, radial_out, mixing, readout, BLOCK
    )
    ghost_rows = ghost * BLOCK

    def ghost_part(number):
        begin = atom_count + number * ghost_rows
        return gradient[:, begin : begin + ghost_rows].reshape(3, ghost, BLOCK)

    face_zero = flow_back(ghost_part(0), -1)
    face_one = flow_back(ghost_part(1), 1)
    low_grad = ghost_part(2)
    high_grad = ghost_part(3)
    low_send_back = jnp.where(low_wrap, sheared_out(low_grad, 1, offset, split), low_grad)
    high_send_back = jnp.where(high_wrap, sheared_out(high_grad, -1, offset, split), high_grad)
    face_two = grad_back(low_send_back, -1)
    face_three = grad_back(high_send_back, 1)
    forces = (-gradient[:, :atom_count]).reshape(3, block_count, BLOCK)
    for number, returned in enumerate((face_zero, face_one, face_two, face_three)):
        selector = block_selector(faces[number], block_count)
        forces = forces - jnp.einsum("kn,pkt->pnt", selector, returned, precision=highest)
    return (energies.reshape(1, atom_count), forces.reshape(3, 1, atom_count))


def solution(mesh):
    in_specs = (
        P(None, "grad", "flow"),
        P("grad", None, "flow"),
        P("grad", None, "flow"),
        P("grad", None, "flow"),
        P(),
        P(),
        P(),
        P(),
        P(),
        P(),
    )
    out_specs = (P("grad", "flow"), P(None, "grad", "flow"))
    return jax.shard_map(body, mesh=mesh, in_specs=in_specs, out_specs=out_specs, check_vma=False)
```

profile of v0, /device:TPU:0, one launch (start us, length us, event | category | flops | bytes accessed | tf_op | source)
XLA Modules:
  0.0 234.2 jit_solution(13269051830490237208)
XLA Ops:
  3.8 3.1 %collective-permute-start.2 = (f32[131,2,128]{2,1,0:T(2,128)S(1)}, f32[131,2,128]{2,1,0:T(2,128)S(1)}, u32[]{:S(2)}, u32[]{:S(2)}) collective-permute-start(f32[131,2,128]{2,1,0:T(2,128)S(1)} %convolution_bitcast_fusion.8), channel_id=1, source_target_pairs={{0,1},{1,2},{2,3},{3,0},{4,5},{5,6},{6,7},{7,4},{8,9},{9,10},{10,1... | collective-permute-start | bytes 402440 | tf_op jit(solution)/shard_map/ppermute | solution.py:17
  9.2 2.7 %collective-permute-start.1 = (f32[131,2,128]{2,1,0:T(2,128)S(1)}, f32[131,2,128]{2,1,0:T(2,128)S(1)}, u32[]{:S(2)}, u32[]{:S(2)}) collective-permute-start(f32[131,2,128]{2,1,0:T(2,128)S(1)} %convolution_bitcast_fusion.9), channel_id=1, source_target_pairs={{0,28},{4,0},{8,4},{12,8},{16,12},{20,16},{24,20},{28,24},{1,29},{... | collective-permute-start | bytes 402440 | tf_op jit(solution)/shard_map/ppermute | solution.py:17
  13.0 2.1 collective-permute-start.7
  18.7 2.7 %collective-permute-start.8 = (f32[131,2,128]{2,1,0:T(2,128)S(1)}, f32[131,2,128]{2,1,0:T(2,128)S(1)}, u32[]{:S(2)}, u32[]{:S(2)}) collective-permute-start(f32[131,2,128]{2,1,0:T(2,128)S(1)} %collective-permute-done.7), channel_id=1, source_target_pairs={{0,28},{4,0},{8,4},{12,8},{16,12},{20,16},{24,20},{28,24},{1,29},{... | collective-permute-start | bytes 402440 | tf_op jit(solution)/shard_map/ppermute | solution.py:17
  21.4 2.5 %collective-permute-done.3 = f32[131,2,128]{2,1,0:T(2,128)S(1)} collective-permute-done((f32[131,2,128]{2,1,0:T(2,128)S(1)}, f32[131,2,128]{2,1,0:T(2,128)S(1)}, u32[]{:S(2)}, u32[]{:S(2)}) %collective-permute-start.3) | collective-permute-done | bytes 134176 | tf_op jit(solution)/shard_map/ppermute | solution.py:17
  24.2 3.0 %collective-permute-start.9 = (f32[131,2,128]{2,1,0:T(2,128)S(1)}, f32[131,2,128]{2,1,0:T(2,128)S(1)}, u32[]{:S(2)}, u32[]{:S(2)}) collective-permute-start(f32[131,2,128]{2,1,0:T(2,128)S(1)} %broadcast_select_fusion), channel_id=1, source_target_pairs={{0,24},{4,28},{8,0},{12,4},{16,8},{20,12},{24,16},{28,20},{1,25},{... | collective-permute-start | bytes 402440 | tf_op jit(solution)/shard_map/ppermute | solution.py:17
  27.1 4.2 %collective-permute-done.4 = f32[131,2,128]{2,1,0:T(2,128)S(1)} collective-permute-done((f32[131,2,128]{2,1,0:T(2,128)S(1)}, f32[131,2,128]{2,1,0:T(2,128)S(1)}, u32[]{:S(2)}, u32[]{:S(2)}) %collective-permute-start.4) | collective-permute-done | bytes 134176 | tf_op jit(solution)/shard_map/ppermute | solution.py:17
  31.5 2.8 %collective-permute-start.5 = (f32[131,2,128]{2,1,0:T(2,128)S(1)}, f32[131,2,128]{2,1,0:T(2,128)S(1)}, u32[]{:S(2)}, u32[]{:S(2)}) collective-permute-start(f32[131,2,128]{2,1,0:T(2,128)S(1)} %broadcast_select_fusion.3), channel_id=1, source_target_pairs={{0,16},{4,20},{8,24},{12,28},{16,0},{20,4},{24,8},{28,12},{1,17},{... | collective-permute-start | bytes 402440 | tf_op jit(solution)/shard_map/ppermute | solution.py:17
  34.4 3.1 %collective-permute-done.5 = f32[131,2,128]{2,1,0:T(2,128)S(1)} collective-permute-done((f32[131,2,128]{2,1,0:T(2,128)S(1)}, f32[131,2,128]{2,1,0:T(2,128)S(1)}, u32[]{:S(2)}, u32[]{:S(2)}) %collective-permute-start.5) | collective-permute-done | bytes 134176 | tf_op jit(solution)/shard_map/ppermute | solution.py:17
  40.4 3.8 %collective-permute-done.6 = f32[131,2,128]{2,1,0:T(2,128)S(1)} collective-permute-done((f32[131,2,128]{2,1,0:T(2,128)S(1)}, f32[131,2,128]{2,1,0:T(2,128)S(1)}, u32[]{:S(2)}, u32[]{:S(2)}) %collective-permute-start.6) | collective-permute-done | bytes 134176 | tf_op jit(solution)/shard_map/ppermute | solution.py:17
  46.1 163.3 %while.67 = (s32[]{:T(128)}, f32[3,1280]{1,0:T(4,128)S(1)}, f32[2,128]{1,0:T(2,128)}, s32[2]{0:T(128)}, s32[32,256]{1,0:T(8,128)S(1)}, /*index=5*/f32[3,1280]{1,...) while((s32[]{:T(128)}, f32[3,1280]{1,0:T(4,128)S(1)}, ...), condition=%wide.region_8.10_spmd, body=%wide.region_0.9_spmd.sunk | while | flops 615754112 | bytes 28353568 | solution.py:132
  48.3 41.4 %while.68 = (s32[]{:T(128)}, f32[9,128,128]{1,0,2:T(8,128)S(1)}, f32[4,3,8,128]{3,2,1,0:T(8,128)S(1)}, f32[4,8,128,128]{3,2,1,0:T(8,128)}, s32[4,8,128]{2,1,0:T(...) while((s32[]{:T(128)}, f32[9,128,128]{1,0,2:T(8,128)S(1)}, ...), condition=%wide.region_2.3_spmd.clone, body=%wide.region_1.2_spmd.clone.sunk | while | flops 170631184 | bytes 6271175 | solution.py:85
  48.3 2.5 %fusion.189 = f32[8,128,3]{1,2,0:T(4,128)S(1)} fusion(s32[8,128]{1,0:T(8,128)S(1)} %bitcast.304, f32[3,1280]{1,0:T(4,128)S(1)} %get-tuple-element.960), kind=kOutput, calls=%fused_computation.2.clone.1 | convolution fusion | flops 48496640 | bytes 31744 | tf_op jit(solution)/shard_map/while/body/eval_jaxpr/while/body/eval_jaxpr/pe,gbe->pgb/dot_general | solution.py:77
  51.6 2.8 %gather_fusion = f32[1024,128]{1,0:T(8,128)S(1)} fusion(f32[1280,128]{1,0:T(8,128)S(1)} %get-tuple-element.964, s32[1024]{0:T(1024)S(1)} %broadcast_clamp_fusion.2), kind=kCustom, calls=%fused_computation.clone.clone.1 | custom fusion | bytes 1052672 | tf_op jit(solution)/shard_map/while/body/eval_jaxpr/while/body/eval_jaxpr/jit(_take)/gather | solution.py:78
  55.6 2.0 fusion.191
  58.7 2.5 %fusion.189 = f32[8,128,3]{1,2,0:T(4,128)S(1)} fusion(s32[8,128]{1,0:T(8,128)S(1)} %bitcast.304, f32[3,1280]{1,0:T(4,128)S(1)} %get-tuple-element.960), kind=kOutput, calls=%fused_computation.2.clone.1 | convolution fusion | flops 48496640 | bytes 31744 | tf_op jit(solution)/shard_map/while/body/eval_jaxpr/while/body/eval_jaxpr/pe,gbe->pgb/dot_general | solution.py:77
  61.9 2.8 %gather_fusion = f32[1024,128]{1,0:T(8,128)S(1)} fusion(f32[1280,128]{1,0:T(8,128)S(1)} %get-tuple-element.964, s32[1024]{0:T(1024)S(1)} %broadcast_clamp_fusion.2), kind=kCustom, calls=%fused_computation.clone.clone.1 | custom fusion | bytes 1052672 | tf_op jit(solution)/shard_map/while/body/eval_jaxpr/while/body/eval_jaxpr/jit(_take)/gather | solution.py:78
  66.0 2.0 fusion.191
  69.0 2.5 %fusion.189 = f32[8,128,3]{1,2,0:T(4,128)S(1)} fusion(s32[8,128]{1,0:T(8,128)S(1)} %bitcast.304, f32[3,1280]{1,0:T(4,128)S(1)} %get-tuple-element.960), kind=kOutput, calls=%fused_computation.2.clone.1 | convolution fusion | flops 48496640 | bytes 31744 | tf_op jit(solution)/shard_map/while/body/eval_jaxpr/while/body/eval_jaxpr/pe,gbe->pgb/dot_general | solution.py:77
  72.3 2.8 %gather_fusion = f32[1024,128]{1,0:T(8,128)S(1)} fusion(f32[1280,128]{1,0:T(8,128)S(1)} %get-tuple-element.964, s32[1024]{0:T(1024)S(1)} %broadcast_clamp_fusion.2), kind=kCustom, calls=%fused_computation.clone.clone.1 | custom fusion | bytes 1052672 | tf_op jit(solution)/shard_map/while/body/eval_jaxpr/while/body/eval_jaxpr/jit(_take)/gather | solution.py:78
  76.3 2.0 fusion.191
  79.3 2.5 %fusion.189 = f32[8,128,3]{1,2,0:T(4,128)S(1)} fusion(s32[8,128]{1,0:T(8,128)S(1)} %bitcast.304, f32[3,1280]{1,0:T(4,128)S(1)} %get-tuple-element.960), kind=kOutput, calls=%fused_computation.2.clone.1 | convolution fusion | flops 48496640 | bytes 31744 | tf_op jit(solution)/shard_map/while/body/eval_jaxpr/while/body/eval_jaxpr/pe,gbe->pgb/dot_general | solution.py:77
  82.6 2.8 %gather_fusion = f32[1024,128]{1,0:T(8,128)S(1)} fusion(f32[1280,128]{1,0:T(8,128)S(1)} %get-tuple-element.964, s32[1024]{0:T(1024)S(1)} %broadcast_clamp_fusion.2), kind=kCustom, calls=%fused_computation.clone.clone.1 | custom fusion | bytes 1052672 | tf_op jit(solution)/shard_map/while/body/eval_jaxpr/while/body/eval_jaxpr/jit(_take)/gather | solution.py:78
  86.6 2.0 fusion.191
  92.0 34.9 %while.69 = (s32[]{:T(128)}, f32[3,128]{0,1:T(8,128)S(1)}, f32[3,1280]{1,0:T(4,128)S(1)}, f32[4,3,8,128]{3,2,1,0:T(8,128)S(1)}, f32[3,128]{1,0:T(4,128)S(1)}, /*...) while((s32[]{:T(128)}, f32[3,128]{0,1:T(8,128)S(1)}, ...), condition=%wide.region_7.8_spmd.clone, body=%wide.region_4.7_spmd.clone.sunk | while | flops 292043008 | bytes 14639884 | solution.py:109
  96.6 1.9 fusion.204
  105.3 1.9 fusion.204
  114.0 1.9 fusion.204
  122.8 1.9 fusion.204
  129.9 41.3 %while.68 = (s32[]{:T(128)}, f32[9,128,128]{1,0,2:T(8,128)S(1)}, f32[4,3,8,128]{3,2,1,0:T(8,128)S(1)}, f32[4,8,128,128]{3,2,1,0:T(8,128)}, s32[4,8,128]{2,1,0:T(...) while((s32[]{:T(128)}, f32[9,128,128]{1,0,2:T(8,128)S(1)}, ...), condition=%wide.region_2.3_spmd.clone, body=%wide.region_1.2_spmd.clone.sunk | while | flops 170631184 | bytes 6271175 | solution.py:85
  129.9 2.5 %fusion.189 = f32[8,128,3]{1,2,0:T(4,128)S(1)} fusion(s32[8,128]{1,0:T(8,128)S(1)} %bitcast.304, f32[3,1280]{1,0:T(4,128)S(1)} %get-tuple-element.960), kind=kOutput, calls=%fused_computation.2.clone.1 | convolution fusion | flops 48496640 | bytes 31744 | tf_op jit(solution)/shard_map/while/body/eval_jaxpr/while/body/eval_jaxpr/pe,gbe->pgb/dot_general | solution.py:77
  133.2 2.8 %gather_fusion = f32[1024,128]{1,0:T(8,128)S(1)} fusion(f32[1280,128]{1,0:T(8,128)S(1)} %get-tuple-element.964, s32[1024]{0:T(1024)S(1)} %broadcast_clamp_fusion.2), kind=kCustom, calls=%fused_computation.clone.clone.1 | custom fusion | bytes 1052672 | tf_op jit(solution)/shard_map/while/body/eval_jaxpr/while/body/eval_jaxpr/jit(_take)/gather | solution.py:78
  137.2 2.0 fusion.191
  140.2 2.5 %fusion.189 = f32[8,128,3]{1,2,0:T(4,128)S(1)} fusion(s32[8,128]{1,0:T(8,128)S(1)} %bitcast.304, f32[3,1280]{1,0:T(4,128)S(1)} %get-tuple-element.960), kind=kOutput, calls=%fused_computation.2.clone.1 | convolution fusion | flops 48496640 | bytes 31744 | tf_op jit(solution)/shard_map/while/body/eval_jaxpr/while/body/eval_jaxpr/pe,gbe->pgb/dot_general | solution.py:77
  143.5 2.8 %gather_fusion = f32[1024,128]{1,0:T(8,128)S(1)} fusion(f32[1280,128]{1,0:T(8,128)S(1)} %get-tuple-element.964, s32[1024]{0:T(1024)S(1)} %broadcast_clamp_fusion.2), kind=kCustom, calls=%fused_computation.clone.clone.1 | custom fusion | bytes 1052672 | tf_op jit(solution)/shard_map/while/body/eval_jaxpr/while/body/eval_jaxpr/jit(_take)/gather | solution.py:78
  147.5 2.0 fusion.191
  150.6 2.5 %fusion.189 = f32[8,128,3]{1,2,0:T(4,128)S(1)} fusion(s32[8,128]{1,0:T(8,128)S(1)} %bitcast.304, f32[3,1280]{1,0:T(4,128)S(1)} %get-tuple-element.960), kind=kOutput, calls=%fused_computation.2.clone.1 | convolution fusion | flops 48496640 | bytes 31744 | tf_op jit(solution)/shard_map/while/body/eval_jaxpr/while/body/eval_jaxpr/pe,gbe->pgb/dot_general | solution.py:77
  153.8 2.8 %gather_fusion = f32[1024,128]{1,0:T(8,128)S(1)} fusion(f32[1280,128]{1,0:T(8,128)S(1)} %get-tuple-element.964, s32[1024]{0:T(1024)S(1)} %broadcast_clamp_fusion.2), kind=kCustom, calls=%fused_computation.clone.clone.1 | custom fusion | bytes 1052672 | tf_op jit(solution)/shard_map/while/body/eval_jaxpr/while/body/eval_jaxpr/jit(_take)/gather | solution.py:78
  157.9 2.0 fusion.191
  160.9 2.5 %fusion.189 = f32[8,128,3]{1,2,0:T(4,128)S(1)} fusion(s32[8,128]{1,0:T(8,128)S(1)} %bitcast.304, f32[3,1280]{1,0:T(4,128)S(1)} %get-tuple-element.960), kind=kOutput, calls=%fused_computation.2.clone.1 | convolution fusion | flops 48496640 | bytes 31744 | tf_op jit(solution)/shard_map/while/body/eval_jaxpr/while/body/eval_jaxpr/pe,gbe->pgb/dot_general | solution.py:77
  164.2 2.8 %gather_fusion = f32[1024,128]{1,0:T(8,128)S(1)} fusion(f32[1280,128]{1,0:T(8,128)S(1)} %get-tuple-element.964, s32[1024]{0:T(1024)S(1)} %broadcast_clamp_fusion.2), kind=kCustom, calls=%fused_computation.clone.clone.1 | custom fusion | bytes 1052672 | tf_op jit(solution)/shard_map/while/body/eval_jaxpr/while/body/eval_jaxpr/jit(_take)/gather | solution.py:78
  168.2 2.0 fusion.191
  173.6 34.9 %while.69 = (s32[]{:T(128)}, f32[3,128]{0,1:T(8,128)S(1)}, f32[3,1280]{1,0:T(4,128)S(1)}, f32[4,3,8,128]{3,2,1,0:T(8,128)S(1)}, f32[3,128]{1,0:T(4,128)S(1)}, /*...) while((s32[]{:T(128)}, f32[3,128]{0,1:T(8,128)S(1)}, ...), condition=%wide.region_7.8_spmd.clone, body=%wide.region_4.7_spmd.clone.sunk | while | flops 292043008 | bytes 14639884 | solution.py:109
  178.1 1.9 fusion.204
  186.8 1.9 fusion.204
  211.8 2.2 collective-permute-start.12
  216.5 2.7 %collective-permute-done.20 = f32[3,2,128]{2,1,0:T(2,128)S(1)} collective-permute-done((f32[3,2,128]{2,1,0:T(2,128)S(1)}, f32[3,2,128]{2,1,0:T(2,128)S(1)}, u32[]{:S(2)}, u32[]{:S(2)}) %collective-permute-start.20) | collective-permute-done | bytes 3104 | tf_op jit(solution)/shard_map/ppermute | solution.py:17
  229.9 2.8 %collective-permute-done.23 = f32[3,2,128]{2,1,0:T(2,128)S(1)} collective-permute-done((f32[3,2,128]{2,1,0:T(2,128)S(1)}, f32[3,2,128]{2,1,0:T(2,128)S(1)}, u32[]{:S(2)}, u32[]{:S(2)}) %collective-permute-start.23) | collective-permute-done | bytes 3104 | tf_op jit(solution)/shard_map/ppermute | solution.py:17
  (576 shorter events, 120.0 us)
Async XLA Ops:
  0.6 17.6 %copy-start.8 = (f32[3,2,128]{2,1,0:T(2,128)S(1)}, f32[3,2,128]{2,1,0:T(2,128)}, u32[]{:S(2)}) copy-start(f32[3,2,128]{2,1,0:T(2,128)} %constant.248.clone.1) | copy-start | bytes 9220
  0.6 17.6 %copy-start.7 = (f32[3,2,128]{2,1,0:T(2,128)S(1)}, f32[3,2,128]{2,1,0:T(2,128)}, u32[]{:S(2)}) copy-start(f32[3,2,128]{2,1,0:T(2,128)} %constant.249.clone.1) | copy-start | bytes 9220
  0.7 15.5 %copy-start.6 = (f32[3,1,256]{2,1,0:T(1,128)S(1)}, f32[3,1,256]{2,1,0:T(1,128)}, u32[]{:S(2)}) copy-start(f32[3,1,256]{2,1,0:T(1,128)} %param.20) | copy-start | bytes 9220
  1.7 19.7 %copy-start.11 = (s32[2]{0:T(128)}, s32[2]{0:T(128)S(1)}, u32[]{:S(2)}) copy-start(s32[2]{0:T(128)S(1)} %get-tuple-element.571) | copy-start | bytes 28
  1.7 19.7 %copy-start.15 = (s32[2]{0:T(128)}, s32[2]{0:T(128)S(1)}, u32[]{:S(2)}) copy-start(s32[2]{0:T(128)S(1)} %get-tuple-element.570) | copy-start | bytes 28
  1.7 29.6 %copy-start.13 = (s32[2]{0:T(128)}, s32[2]{0:T(128)S(1)}, u32[]{:S(2)}) copy-start(s32[2]{0:T(128)S(1)} %get-tuple-element.569) | copy-start | bytes 28
  1.7 29.6 %copy-start.14 = (s32[2]{0:T(128)}, s32[2]{0:T(128)S(1)}, u32[]{:S(2)}) copy-start(s32[2]{0:T(128)S(1)} %get-tuple-element.572) | copy-start | bytes 28
  3.8 14.6 %collective-permute-start.2 = (f32[131,2,128]{2,1,0:T(2,128)S(1)}, f32[131,2,128]{2,1,0:T(2,128)S(1)}, u32[]{:S(2)}, u32[]{:S(2)}) collective-permute-start(f32[131,2,128]{2,1,0:T(2,128)S(1)} %convolution_bitcast_fusion.8), channel_id=1, source_target_pairs={{0,1},{1,2},{2,3},{3,0},{4,5},{5,6},{6,7},{7,4},{8,9},{9,10},{10,1... | collective-permute-start | bytes 402440 | tf_op jit(solution)/shard_map/ppermute | solution.py:17
  8.0 10.2 %collective-permute-start = (f32[131,2,128]{2,1,0:T(2,128)S(1)}, f32[131,2,128]{2,1,0:T(2,128)S(1)}, u32[]{:S(2)}, u32[]{:S(2)}) collective-permute-start(f32[131,2,128]{2,1,0:T(2,128)S(1)} %convolution_bitcast_fusion.10), channel_id=1, source_target_pairs={{0,4},{4,8},{8,12},{12,16},{16,20},{20,24},{24,28},{28,0},{1,5},{5... | collective-permute-start | bytes 402440 | tf_op jit(solution)/shard_map/ppermute | solution.py:17
  9.2 9.1 %collective-permute-start.1 = (f32[131,2,128]{2,1,0:T(2,128)S(1)}, f32[131,2,128]{2,1,0:T(2,128)S(1)}, u32[]{:S(2)}, u32[]{:S(2)}) collective-permute-start(f32[131,2,128]{2,1,0:T(2,128)S(1)} %convolution_bitcast_fusion.9), channel_id=1, source_target_pairs={{0,28},{4,0},{8,4},{12,8},{16,12},{20,16},{24,20},{28,24},{1,29},{... | collective-permute-start | bytes 402440 | tf_op jit(solution)/shard_map/ppermute | solution.py:17
  13.0 5.7 %collective-permute-start.7 = (f32[131,2,128]{2,1,0:T(2,128)S(1)}, f32[131,2,128]{2,1,0:T(2,128)S(1)}, u32[]{:S(2)}, u32[]{:S(2)}) collective-permute-start(f32[131,2,128]{2,1,0:T(2,128)S(1)} %convolution_bitcast_fusion.7), channel_id=1, source_target_pairs={{0,3},{1,0},{2,1},{3,2},{4,7},{5,4},{6,5},{7,6},{8,11},{9,8},{10,9... | collective-permute-start | bytes 402440 | tf_op jit(solution)/shard_map/ppermute | solution.py:17
  16.8 27.9 %copy-start.9 = (pred[2]{0:T(512)(128)(4,1)}, pred[2]{0:T(512)(128)(4,1)S(1)}, u32[]{:S(2)}) copy-start(pred[2]{0:T(512)(128)(4,1)S(1)} %iota_compare_fusion.9) | copy-start | bytes 10
  18.5 5.5 %collective-permute-start.3 = (f32[131,2,128]{2,1,0:T(2,128)S(1)}, f32[131,2,128]{2,1,0:T(2,128)S(1)}, u32[]{:S(2)}, u32[]{:S(2)}) collective-permute-start(f32[131,2,128]{2,1,0:T(2,128)S(1)} %collective-permute-done.2), channel_id=1, source_target_pairs={{0,4},{4,8},{8,12},{12,16},{16,20},{20,24},{24,28},{28,0},{1,5},{5... | collective-permute-start | bytes 402440 | tf_op jit(solution)/shard_map/ppermute | solution.py:17
  18.7 5.4 %collective-permute-start.8 = (f32[131,2,128]{2,1,0:T(2,128)S(1)}, f32[131,2,128]{2,1,0:T(2,128)S(1)}, u32[]{:S(2)}, u32[]{:S(2)}) collective-permute-start(f32[131,2,128]{2,1,0:T(2,128)S(1)} %collective-permute-done.7), channel_id=1, source_target_pairs={{0,28},{4,0},{8,4},{12,8},{16,12},{20,16},{24,20},{28,24},{1,29},{... | collective-permute-start | bytes 402440 | tf_op jit(solution)/shard_map/ppermute | solution.py:17
  24.0 7.3 %collective-permute-start.4 = (f32[131,2,128]{2,1,0:T(2,128)S(1)}, f32[131,2,128]{2,1,0:T(2,128)S(1)}, u32[]{:S(2)}, u32[]{:S(2)}) collective-permute-start(f32[131,2,128]{2,1,0:T(2,128)S(1)} %broadcast_select_fusion.1), channel_id=1, source_target_pairs={{0,8},{4,12},{8,16},{12,20},{16,24},{20,28},{24,0},{28,4},{1,9},{5... | collective-permute-start | bytes 402440 | tf_op jit(solution)/shard_map/ppermute | solution.py:17
  24.2 10.1 %collective-permute-start.9 = (f32[131,2,128]{2,1,0:T(2,128)S(1)}, f32[131,2,128]{2,1,0:T(2,128)S(1)}, u32[]{:S(2)}, u32[]{:S(2)}) collective-permute-start(f32[131,2,128]{2,1,0:T(2,128)S(1)} %broadcast_select_fusion), channel_id=1, source_target_pairs={{0,24},{4,28},{8,0},{12,4},{16,8},{20,12},{24,16},{28,20},{1,25},{... | collective-permute-start | bytes 402440 | tf_op jit(solution)/shard_map/ppermute | solution.py:17
  31.3 14.7 %copy-start.1 = (f32[64,128]{1,0:T(8,128)S(1)}, f32[64,128]{1,0:T(8,128)}, u32[]{:S(2)}) copy-start(f32[64,128]{1,0:T(8,128)} %param.27) | copy-start | bytes 98308
  31.3 14.7 %copy-start.3 = (f32[8,64]{1,0:T(8,128)S(1)}, f32[8,64]{1,0:T(8,128)}, u32[]{:S(2)}) copy-start(f32[8,64]{1,0:T(8,128)} %param.26) | copy-start | bytes 6148
  31.3 14.7 %copy-start.4 = (s32[1,32,256]{2,1,0:T(8,128)S(1)}, s32[1,32,256]{2,1,0:T(8,128)}, u32[]{:S(2)}) copy-start(s32[1,32,256]{2,1,0:T(8,128)} %param.22) | copy-start | bytes 98308
  31.4 14.7 %copy-start.5 = (f32[128]{0:T(128)S(1)}, f32[128]{0:T(128)}, u32[]{:S(2)}) copy-start(f32[128]{0:T(128)} %param.29) | copy-start | bytes 1540
  31.5 6.0 %collective-permute-start.5 = (f32[131,2,128]{2,1,0:T(2,128)S(1)}, f32[131,2,128]{2,1,0:T(2,128)S(1)}, u32[]{:S(2)}, u32[]{:S(2)}) collective-permute-start(f32[131,2,128]{2,1,0:T(2,128)S(1)} %broadcast_select_fusion.3), channel_id=1, source_target_pairs={{0,16},{4,20},{8,24},{12,28},{16,0},{20,4},{24,8},{28,12},{1,17},{... | collective-permute-start | bytes 402440 | tf_op jit(solution)/shard_map/ppermute | solution.py:17
  34.3 5.1 %collective-permute-start.10 = (f32[131,2,128]{2,1,0:T(2,128)S(1)}, f32[131,2,128]{2,1,0:T(2,128)S(1)}, u32[]{:S(2)}, u32[]{:S(2)}) collective-permute-start(f32[131,2,128]{2,1,0:T(2,128)S(1)} %broadcast_select_fusion.2), channel_id=1, source_target_pairs={{0,16},{4,20},{8,24},{12,28},{16,0},{20,4},{24,8},{28,12},{1,17},{... | collective-permute-start | bytes 402440 | tf_op jit(solution)/shard_map/ppermute | solution.py:17
  37.5 6.6 %collective-permute-start.6 = (f32[131,2,128]{2,1,0:T(2,128)S(1)}, f32[131,2,128]{2,1,0:T(2,128)S(1)}, u32[]{:S(2)}, u32[]{:S(2)}) collective-permute-start(f32[131,2,128]{2,1,0:T(2,128)S(1)} %broadcast_select_fusion.5), channel_id=1, source_target_pairs={{0,4},{4,8},{8,12},{12,16},{16,20},{20,24},{24,28},{28,0},{1,5},{5... | collective-permute-start | bytes 402440 | tf_op jit(solution)/shard_map/ppermute | solution.py:17
  39.4 5.3 %collective-permute-start.11 = (f32[131,2,128]{2,1,0:T(2,128)S(1)}, f32[131,2,128]{2,1,0:T(2,128)S(1)}, u32[]{:S(2)}, u32[]{:S(2)}) collective-permute-start(f32[131,2,128]{2,1,0:T(2,128)S(1)} %broadcast_select_fusion.4), channel_id=1, source_target_pairs={{0,28},{4,0},{8,4},{12,8},{16,12},{20,16},{24,20},{28,24},{1,29},{... | collective-permute-start | bytes 402440 | tf_op jit(solution)/shard_map/ppermute | solution.py:17
  46.1 165.0 %copy-start.10 = (pred[2]{0:T(512)(128)(4,1)S(1)}, pred[2]{0:T(512)(128)(4,1)}, u32[]{:S(2)}) copy-start(pred[2]{0:T(512)(128)(4,1)} %copy-done.9) | copy-start | bytes 10
  46.1 187.4 %copy-start.12 = (s32[2]{0:T(128)S(1)}, s32[2]{0:T(128)}, u32[]{:S(2)}) copy-start(s32[2]{0:T(128)} %copy-done.11) | copy-start | bytes 28
  92.0 35.2 %copy-start.16 = (f32[2,128]{1,0:T(2,128)S(1)}, f32[2,128]{1,0:T(2,128)}, u32[]{:S(2)}) copy-start(f32[2,128]{1,0:T(2,128)} %get-tuple-element.1025) | copy-start | bytes 3076 | tf_op jit(solution)/shard_map/while
  92.4 1.6 copy-start
  101.1 1.6 copy-start
  109.9 1.6 copy-start
  118.6 1.6 copy-start
  173.5 35.2 %copy-start.16 = (f32[2,128]{1,0:T(2,128)S(1)}, f32[2,128]{1,0:T(2,128)}, u32[]{:S(2)}) copy-start(f32[2,128]{1,0:T(2,128)} %get-tuple-element.1025) | copy-start | bytes 3076 | tf_op jit(solution)/shard_map/while
  174.0 1.6 copy-start
  182.7 1.6 copy-start
  191.4 1.6 copy-start
  200.1 1.6 copy-start
  210.1 3.9 %collective-permute-start.14 = (f32[3,2,128]{2,1,0:T(2,128)S(1)}, f32[3,2,128]{2,1,0:T(2,128)S(1)}, u32[]{:S(2)}, u32[]{:S(2)}) collective-permute-start(f32[3,2,128]{2,1,0:T(2,128)S(1)} %fusion.111), channel_id=1, source_target_pairs={{0,28},{4,0},{8,4},{12,8},{16,12},{20,16},{24,20},{28,24},{1,29},{... | collective-permute-start | bytes 9224 | tf_op jit(solution)/shard_map/ppermute | solution.py:17
  211.2 4.0 %collective-permute-start.19 = (f32[3,2,128]{2,1,0:T(2,128)S(1)}, f32[3,2,128]{2,1,0:T(2,128)S(1)}, u32[]{:S(2)}, u32[]{:S(2)}) collective-permute-start(f32[3,2,128]{2,1,0:T(2,128)S(1)} %fusion.108), channel_id=1, source_target_pairs={{0,4},{4,8},{8,12},{12,16},{16,20},{20,24},{24,28},{28,0},{1,5},{5... | collective-permute-start | bytes 9224 | tf_op jit(solution)/shard_map/ppermute | solution.py:17
  211.3 4.0 %collective-permute-start.13 = (f32[3,2,128]{2,1,0:T(2,128)S(1)}, f32[3,2,128]{2,1,0:T(2,128)S(1)}, u32[]{:S(2)}, u32[]{:S(2)}) collective-permute-start(f32[3,2,128]{2,1,0:T(2,128)S(1)} %reshape.216), channel_id=1, source_target_pairs={{0,4},{4,8},{8,12},{12,16},{16,20},{20,24},{24,28},{28,0},{1,5},{5... | collective-permute-start | bytes 9224 | tf_op jit(solution)/shard_map/ppermute | solution.py:17
  211.8 21.7 %collective-permute-start.12 = (f32[3,2,128]{2,1,0:T(2,128)S(1)}, f32[3,2,128]{2,1,0:T(2,128)S(1)}, u32[]{:S(2)}, u32[]{:S(2)}) collective-permute-start(f32[3,2,128]{2,1,0:T(2,128)S(1)} %reshape.215), channel_id=1, source_target_pairs={{0,28},{4,0},{8,4},{12,8},{16,12},{20,16},{24,20},{28,24},{1,29},{... | collective-permute-start | bytes 9224 | tf_op jit(solution)/shard_map/ppermute | solution.py:17
  214.1 2.4 %collective-permute-start.15 = (f32[3,2,128]{2,1,0:T(2,128)S(1)}, f32[3,2,128]{2,1,0:T(2,128)S(1)}, u32[]{:S(2)}, u32[]{:S(2)}) collective-permute-start(f32[3,2,128]{2,1,0:T(2,128)S(1)} %fusion.113), channel_id=1, source_target_pairs={{0,28},{4,0},{8,4},{12,8},{16,12},{20,16},{24,20},{28,24},{1,29},{... | collective-permute-start | bytes 9224 | tf_op jit(solution)/shard_map/ppermute | solution.py:17
  215.2 4.0 %collective-permute-start.20 = (f32[3,2,128]{2,1,0:T(2,128)S(1)}, f32[3,2,128]{2,1,0:T(2,128)S(1)}, u32[]{:S(2)}, u32[]{:S(2)}) collective-permute-start(f32[3,2,128]{2,1,0:T(2,128)S(1)} %fusion.110), channel_id=1, source_target_pairs={{0,4},{4,8},{8,12},{12,16},{16,20},{20,24},{24,28},{28,0},{1,5},{5... | collective-permute-start | bytes 9224 | tf_op jit(solution)/shard_map/ppermute | solution.py:17
  216.4 3.6 %collective-permute-start.16 = (f32[3,2,128]{2,1,0:T(2,128)S(1)}, f32[3,2,128]{2,1,0:T(2,128)S(1)}, u32[]{:S(2)}, u32[]{:S(2)}) collective-permute-start(f32[3,2,128]{2,1,0:T(2,128)S(1)} %broadcast_select_fusion.11), channel_id=1, source_target_pairs={{0,24},{4,28},{8,0},{12,4},{16,8},{20,12},{24,16},{28,20},{1,25},{... | collective-permute-start | bytes 9224 | tf_op jit(solution)/shard_map/ppermute | solution.py:17
  219.2 4.5 %collective-permute-start.21 = (f32[3,2,128]{2,1,0:T(2,128)S(1)}, f32[3,2,128]{2,1,0:T(2,128)S(1)}, u32[]{:S(2)}, u32[]{:S(2)}) collective-permute-start(f32[3,2,128]{2,1,0:T(2,128)S(1)} %broadcast_select_fusion.10), channel_id=1, source_target_pairs={{0,8},{4,12},{8,16},{12,20},{16,24},{20,28},{24,0},{28,4},{1,9},{5... | collective-permute-start | bytes 9224 | tf_op jit(solution)/shard_map/ppermute | solution.py:17
  220.0 5.4 %collective-permute-start.17 = (f32[3,2,128]{2,1,0:T(2,128)S(1)}, f32[3,2,128]{2,1,0:T(2,128)S(1)}, u32[]{:S(2)}, u32[]{:S(2)}) collective-permute-start(f32[3,2,128]{2,1,0:T(2,128)S(1)} %broadcast_select_fusion.13), channel_id=1, source_target_pairs={{0,16},{4,20},{8,24},{12,28},{16,0},{20,4},{24,8},{28,12},{1,17},{... | collective-permute-start | bytes 9224 | tf_op jit(solution)/shard_map/ppermute | solution.py:17
  223.7 3.6 %collective-permute-start.22 = (f32[3,2,128]{2,1,0:T(2,128)S(1)}, f32[3,2,128]{2,1,0:T(2,128)S(1)}, u32[]{:S(2)}, u32[]{:S(2)}) collective-permute-start(f32[3,2,128]{2,1,0:T(2,128)S(1)} %broadcast_select_fusion.12), channel_id=1, source_target_pairs={{0,16},{4,20},{8,24},{12,28},{16,0},{20,4},{24,8},{28,12},{1,17},{... | collective-permute-start | bytes 9224 | tf_op jit(solution)/shard_map/ppermute | solution.py:17
  225.4 3.6 %collective-permute-start.18 = (f32[3,2,128]{2,1,0:T(2,128)S(1)}, f32[3,2,128]{2,1,0:T(2,128)S(1)}, u32[]{:S(2)}, u32[]{:S(2)}) collective-permute-start(f32[3,2,128]{2,1,0:T(2,128)S(1)} %select_select_fusion.1), channel_id=1, source_target_pairs={{0,3},{1,0},{2,1},{3,2},{4,7},{5,4},{6,5},{7,6},{8,11},{9,8},{10,9... | collective-permute-start | bytes 9224 | tf_op jit(solution)/shard_map/ppermute | solution.py:17
  227.3 5.4 %collective-permute-start.23 = (f32[3,2,128]{2,1,0:T(2,128)S(1)}, f32[3,2,128]{2,1,0:T(2,128)S(1)}, u32[]{:S(2)}, u32[]{:S(2)}) collective-permute-start(f32[3,2,128]{2,1,0:T(2,128)S(1)} %select_select_fusion), channel_id=1, source_target_pairs={{0,1},{1,2},{2,3},{3,0},{4,5},{5,6},{6,7},{7,4},{8,9},{9,10},{10,1... | collective-permute-start | bytes 9224 | tf_op jit(solution)/shard_map/ppermute | solution.py:17
  (4 other events, 3.0 us)
where the time goes:
time: 235 us; the launch traced here: 234 us
  matrix products  113 us (48%)
  local copies, waits for them, and re-layouts  47.4 us (20%)
  starting transfers between devices  27.6 us (12%)
  waiting for transfers between devices  26.1 us (11%)
  other arithmetic  13.5 us (6%)
  loops' own time  4.22 us (2%)
  between operations  2.48 us (1%)
    dot_general x24, matrix products, contribution(): return jnp.einsum('gbc,mgb->mcb', weighted, harmonic, precision=highest)  39.5 us
    ppermute x24, starting transfers between devices, from_behind(): return lax.ppermute(x, axis, [(i, (i + by) % peers) for i in range(peers)])  27.6 us
    ppermute x24, waiting for transfers between devices, from_behind(): return lax.ppermute(x, axis, [(i, (i + by) % peers) for i in range(peers)])  26.1 us
    gather x8, local copies, waits for them, and re-layouts, forward(): jnp.take(feat_rows, group_idx.reshape(-1), axis=0)  22.5 us
    dot_general x24, matrix products, contribution(): radial = jnp.einsum('hc,hgb->gbc', radial_out, hidden, precision=highest)  19.9 us
    dot_general x8, matrix products, forward(): group_pos = jnp.einsum('pe,gbe->pgb', ext_pos, selector, precision=highest)  19.7 us
    dot_general x8, matrix products, backward(): jnp.einsum('pgb,gbe->pe', group_grad, selector, precision=highest)  14.5 us
    dot_general x24, matrix products, contribution(): jnp.einsum('rh,rgb->hgb', radial_in, gaussians, precision=highest)  10 us
  transfers between devices with their start and end apart: 24, of which 13 were waited for; matrix products, arithmetic and copies ran while one was open for 4% of the time, Pallas kernels for 0%

commit v1 on v0

v1 whole, which is shorter than its diff:
```python
import functools

import jax
import jax.numpy as jnp
from jax import lax
from jax.experimental import pallas as pl
from jax.experimental.pallas import tpu as pltpu
from jax.sharding import PartitionSpec as P

LANES = 128
GROUPS = 8
highest = lax.Precision.HIGHEST
root_three = 3.0**0.5
root_five = 5.0**0.5
root_fifteen = 15.0**0.5
f32 = jnp.float32
bf16 = jnp.bfloat16


def halves(value):
    upper = value.astype(bf16).astype(f32)
    return upper, value - upper


def nt(left, right, precision=None):
    return lax.dot_general(left, right, (((1,), (1,)), ((), ())), precision=precision, preferred_element_type=f32)


def core_kernel(groups, neighbours, number, rows, ghost, split_ref, row_ref, idx_ref, own_pos, own_feat,
                win_ref, wout_ref, mix_ref, read_ref, left_ref, right_ref, *refs):
    slot_refs, refs = refs[: 2 * ghost], refs[2 * ghost :]
    energy_ref, own_ref, ghost_ref = refs[:3]
    xyz_scr, d_scr, w_scr, dw_scr, mom_scr, g_scr, acc_scr, cen_scr = refs[3:]
    split = split_ref[0]
    row = row_ref[0]
    atoms = own_pos.shape[1]
    channels = own_feat.shape[0]
    hidden = win_ref.shape[1]
    tile = groups * neighbours
    tiles = atoms // groups
    own_chunks = atoms // LANES
    faces = 4
    chunks = own_chunks + faces * ghost
    factor = neighbours ** (-0.5)
    ghosts = [left_ref.at[j] for j in range(ghost)] + [right_ref.at[j] for j in range(ghost)] + list(slot_refs)

    def pos_chunk(c, axis):
        if c < own_chunks:
            return own_pos[axis : axis + 1, c * LANES : (c + 1) * LANES]
        k, j = divmod(c - own_chunks, ghost)
        line = ghosts[c - own_chunks][channels + axis : channels + axis + 1, :]
        fraction = split.astype(f32) / ghost
        if axis == 0:
            if k < 2:
                line = line + (2.0 * k - 1.0)
            elif k == 2:
                line = line + jnp.where(row == 0, jnp.where(j < split, fraction - 1.0, fraction), 0.0)
            else:
                line = line + jnp.where(
                    row == rows - 1, jnp.where(j < ghost - split, -fraction, 1.0 - fraction), 0.0
                )
        elif axis == 1 and k >= 2:
            line = line + (2.0 * k - 5.0)
        return line

    def feat_chunk(c):
        if c < own_chunks:
            return own_feat[:, c * LANES : (c + 1) * LANES]
        return ghosts[c - own_chunks][0:channels, :]

    blocks = tile // LANES
    for lb in range(blocks):
        lanes = slice(lb * LANES, (lb + 1) * LANES)
        idx = idx_ref[:, lanes]
        low = jnp.bitwise_and(idx, LANES - 1)
        chunk = jnp.right_shift(idx, LANES.bit_length() - 1)
        lines = lax.broadcasted_iota(jnp.int32, idx.shape, 0)
        cols = lax.broadcasted_iota(jnp.int32, idx.shape, 1) + lb * LANES
        centre = lines * groups + cols // neighbours
        clow = jnp.bitwise_and(centre, LANES - 1)
        cchunk = jnp.right_shift(centre, LANES.bit_length() - 1)
        for axis in range(3):
            other = None
            mine = None
            for c in range(chunks):
                src = jnp.broadcast_to(pos_chunk(c, axis), idx.shape)
                got = jnp.take_along_axis(src, low, axis=1)
                other = got if other is None else jnp.where(chunk == c, got, other)
                if c < own_chunks:
                    got = jnp.take_along_axis(src, clow, axis=1)
                    mine = got if mine is None else jnp.where(cchunk == c, got, mine)
            xyz_scr[axis, :, lanes] = other - mine

    d_scr[...] = jnp.zeros(d_scr.shape, f32)
    d_scr[0:number, 0:hidden] = win_ref[...]
    d_scr[number : 2 * number, hidden : 2 * hidden] = win_ref[...]
    dhi, dlo = halves(d_scr[...])
    first = jnp.transpose(jnp.concatenate([dhi, dhi, dlo, dlo], axis=0)).astype(bf16)
    ohi, olo = halves(wout_ref[...])
    second = jnp.transpose(jnp.concatenate([ohi, ohi, olo, olo], axis=0)).astype(bf16)

    row_iota = lax.broadcasted_iota(jnp.int32, (groups, tile), 0)
    lane_iota = lax.broadcasted_iota(jnp.int32, (groups, tile), 1)
    mine_mask = row_iota == lane_iota // neighbours
    centres = row_iota.astype(f32) * (6.0 / (number - 1))

    def spread(axis, t):
        return jnp.broadcast_to(xyz_scr[axis, pl.ds(t, 1), :], (groups, tile))

    def harmonics(x, y, z):
        square = x * x + y * y + z * z
        values = [
            jnp.ones_like(x),
            root_three * x,
            root_three * y,
            root_three * z,
            root_fifteen * x * y,
            root_fifteen * y * z,
            0.5 * root_five * (3.0 * z * z - square),
            root_fifteen * x * z,
            0.5 * root_fifteen * (x * x - y * y),
        ]
        return values, square

    def forward(t, carry):
        x, y, z = spread(0, t), spread(1, t), spread(2, t)
        values, square = harmonics(x, y, z)
        away = square - centres
        scaled = away / 0.75
        gauss = jnp.exp(-0.5 * (scaled * scaled))
        slope = gauss * (away * (-1.0 / 0.5625))
        bhi, blo = halves(jnp.concatenate([gauss, slope], axis=0))
        basis = jnp.concatenate([bhi, blo, bhi, blo], axis=0).astype(bf16)
        both = jnp.dot(first, basis, preferred_element_type=f32)
        h, dh = both[0:hidden], both[hidden : 2 * hidden]
        sig = 0.5 * jnp.tanh(0.5 * h) + 0.5
        act = h * sig
        dact = dh * (sig + act * (1.0 - sig))
        ahi, alo = halves(act)
        acts = jnp.concatenate([ahi, alo, ahi, alo], axis=0).astype(bf16)
        chi, clo = halves(dact)
        dacts = jnp.concatenate([chi, clo, chi, clo], axis=0).astype(bf16)
        radial = jnp.dot(second, acts, preferred_element_type=f32)
        dradial = jnp.dot(second, dacts, preferred_element_type=f32)
        idx_row = idx_ref[pl.ds(t, 1), :]
        for lb in range(blocks):
            lanes = slice(lb * LANES, (lb + 1) * LANES)
            idx = jnp.broadcast_to(idx_row[:, lanes], (channels, LANES))
            low = jnp.bitwise_and(idx, LANES - 1)
            chunk = jnp.right_shift(idx, LANES.bit_length() - 1)
            feat = None
            for c in range(chunks):
                got = jnp.take_along_axis(feat_chunk(c), low, axis=1)
                feat = got if feat is None else jnp.where(chunk == c, got, feat)
            whi, wlo = halves(radial[:, lanes] * feat)
            w_scr[t, 0:channels, lanes] = whi.astype(bf16)
            w_scr[t, channels : 2 * channels, lanes] = wlo.astype(bf16)
            whi, wlo = halves(dradial[:, lanes] * feat)
            dw_scr[t, 0:channels, lanes] = whi.astype(bf16)
            dw_scr[t, channels : 2 * channels, lanes] = wlo.astype(bf16)
        his, los = [], []
        for value in values:
            hi, lo = halves(jnp.where(mine_mask, value, 0.0))
            his.append(hi)
            los.append(lo)
        ys = jnp.concatenate(his + los, axis=0).astype(bf16)
        out = nt(ys, w_scr[t])
        n = len(values) * groups
        total = (out[0:n, 0:channels] + out[0:n, channels:]) + out[n : 2 * n, 0:channels]
        base = pl.multiple_of(t * groups, groups)
        for m in range(len(values)):
            mom_scr[m, pl.ds(base, groups), :] = total[m * groups : (m + 1) * groups] * factor
        return carry

    lax.fori_loop(0, tiles, forward, 0)

    degree = [0, 1, 1, 1, 2, 2, 2, 2, 2]
    count = len(degree)
    invariants = []
    for l in range(3):
        total = None
        for m in range(count):
            if degree[m] == l:
                sq = mom_scr[m] * mom_scr[m]
                total = sq if total is None else total + sq
        invariants.append(total)
    mixed = None
    for l in range(3):
        part = jnp.dot(invariants[l], mix_ref[l], precision=highest, preferred_element_type=f32)
        mixed = part if mixed is None else mixed + part
    sig = 0.5 * jnp.tanh(0.5 * mixed) + 0.5
    act = mixed * sig
    reads = read_ref[...]
    energy_ref[...] = nt(jnp.broadcast_to(reads, (8, channels)), act, highest)[0:1]
    dmixed = reads * (sig + act * (1.0 - sig))
    for l in range(3):
        dinv = nt(dmixed, mix_ref[l], highest) * (2.0 * factor)
        for m in range(count):
            if degree[m] == l:
                hi, lo = halves(dinv * mom_scr[m])
                g_scr[:, m * groups : (m + 1) * groups, :] = hi.reshape(tiles, groups, channels)
                g_scr[:, (count + m) * groups : (count + m + 1) * groups, :] = lo.reshape(tiles, groups, channels)

    acc_scr[...] = jnp.zeros(acc_scr.shape, f32)
    padded = acc_scr.shape[0] // 6
    chunk_iota = lax.broadcasted_iota(jnp.int32, (padded, tile), 0)
    lane_rows = lax.broadcasted_iota(jnp.int32, (LANES, tile), 0)
    n = count * groups

    def backward(t, carry):
        x, y, z = spread(0, t), spread(1, t), spread(2, t)
        values, _ = harmonics(x, y, z)
        g = g_scr[t]
        gl = jnp.concatenate(
            [g.astype(bf16), jnp.concatenate([g[0:n], jnp.zeros((n, channels), f32)], axis=0).astype(bf16)], axis=1
        )
        a = jnp.dot(gl, w_scr[t], preferred_element_type=f32)
        b = jnp.dot(gl, dw_scr[t], preferred_element_type=f32)
        A = [a[m * groups : (m + 1) * groups] + a[n + m * groups : n + (m + 1) * groups] for m in range(count)]
        rad = None
        for m in range(count):
            B = b[m * groups : (m + 1) * groups] + b[n + m * groups : n + (m + 1) * groups]
            rad = B if m == 0 else rad + values[m] * B
        rad = 2.0 * rad
        dx = root_three * A[1] + root_fifteen * (y * A[4] + z * A[7] + x * A[8]) - root_five * (x * A[6]) + x * rad
        dy = root_three * A[2] + root_fifteen * (x * A[4] + z * A[5] - y * A[8]) - root_five * (y * A[6]) + y * rad
        dz = root_three * A[3] + root_fifteen * (y * A[5] + x * A[7]) + (2.0 * root_five) * (z * A[6]) + z * rad
        comps = [jnp.where(mine_mask, v, 0.0) for v in (dx, dy, dz)]
        base = pl.multiple_of(t * groups, groups)
        lane = lax.broadcasted_iota(jnp.int32, (groups, LANES), 1)
        cen = jnp.zeros((groups, LANES), f32)
        for i, v in enumerate(comps):
            cen = jnp.where(lane == i, jnp.sum(v, axis=1, keepdims=True), cen)
        cen_scr[pl.ds(base, groups), :] = cen
        idx = idx_ref[pl.ds(t, 1), :]
        low = jnp.bitwise_and(idx, LANES - 1)
        chunk = jnp.right_shift(idx, LANES.bit_length() - 1)
        hit = jnp.broadcast_to(chunk, (padded, tile)) == chunk_iota
        his, los = [], []
        for v in comps:
            row = jnp.sum(v, axis=0, keepdims=True)
            hi, lo = halves(jnp.where(hit, jnp.broadcast_to(row, (padded, tile)), 0.0))
            his.append(hi)
            los.append(lo)
        left = jnp.concatenate(his + los, axis=0).astype(bf16)
        right = jnp.where(jnp.broadcast_to(low, (LANES, tile)) == lane_rows, 1.0, 0.0).astype(bf16)
        acc_scr[...] += nt(left, right)
        return carry

    lax.fori_loop(0, tiles, backward, 0)

    half = 3 * padded
    cen = jnp.concatenate(
        [jnp.transpose(cen_scr[c * LANES : (c + 1) * LANES, :])[0:8] for c in range(own_chunks)], axis=1
    )
    for axis in range(3):
        lo = axis * padded
        rows = acc_scr[lo : lo + padded] + acc_scr[half + lo : half + lo + padded]
        for c in range(own_chunks):
            own_ref[axis : axis + 1, c * LANES : (c + 1) * LANES] = (
                rows[c : c + 1] - cen[axis : axis + 1, c * LANES : (c + 1) * LANES]
            )
        for k in range(faces):
            for j in range(ghost):
                c = own_chunks + k * ghost + j
                ghost_ref[k, j, axis : axis + 1, :] = rows[c : c + 1]


def core(split, row, idx, own_pos, own_feat, win, wout, mixing, readout, left, right, slots, rows):
    atoms = own_pos.shape[1]
    channels = own_feat.shape[0]
    tiles, tile = idx.shape
    groups = GROUPS
    neighbours = tile // groups
    ghost = left.shape[0]
    faces = 4
    number, hidden = win.shape
    chunks = atoms // LANES + faces * ghost
    padded = -(-chunks // 16) * 16
    vm = pl.BlockSpec(memory_space=pltpu.VMEM)
    sm = pl.BlockSpec(memory_space=pltpu.SMEM)
    return pl.pallas_call(
        functools.partial(core_kernel, groups, neighbours, number, rows, ghost),
        out_shape=(
            jax.ShapeDtypeStruct((1, atoms), f32),
            jax.ShapeDtypeStruct((3, atoms), f32),
            jax.ShapeDtypeStruct((faces, ghost, 3, LANES), f32),
        ),
        in_specs=[sm, sm] + [vm] * (9 + 2 * ghost),
        out_specs=(vm, vm, vm),
        scratch_shapes=[
            pltpu.VMEM((3, tiles, tile), f32),
            pltpu.VMEM((2 * number, 2 * hidden), f32),
            pltpu.VMEM((tiles, 2 * channels, tile), bf16),
            pltpu.VMEM((tiles, 2 * channels, tile), bf16),
            pltpu.VMEM((9, atoms, channels), f32),
            pltpu.VMEM((tiles, 18 * groups, channels), f32),
            pltpu.VMEM((6 * padded, LANES), f32),
            pltpu.VMEM((atoms, LANES), f32),
        ],
        compiler_params=pltpu.CompilerParams(vmem_limit_bytes=32 << 20),
        name="core",
    )(split, row, idx, own_pos, own_feat, win, wout, mixing, readout, left, right, *slots)


def source_slot(slot, ghost, crossing, split, sign):
    rolled = lax.rem(slot + sign * split + ghost, ghost)
    return jnp.where(crossing, rolled, slot)


def pack_kernel(rows, split_ref, row_ref, faces_ref, pos_ref, feat_ref, left_ref, right_ref, *slot_refs):
    ghost = faces_ref.shape[1]
    channels = feat_ref.shape[0]
    split = split_ref[0]
    row = row_ref[0]

    def put(dest, block):
        lanes = pl.ds(pl.multiple_of(block * LANES, LANES), LANES)
        dest[0:channels, :] = feat_ref[:, lanes]
        dest[channels : channels + 3, :] = pos_ref[:, lanes]
        dest[channels + 3 :, :] = jnp.zeros((dest.shape[0] - channels - 3, LANES), f32)

    for j in range(ghost):
        put(left_ref.at[j], faces_ref[0, j])
        put(right_ref.at[j], faces_ref[1, j])
        put(slot_refs[j], faces_ref[2, source_slot(j, ghost, row == rows - 1, split, -1)])
        put(slot_refs[ghost + j], faces_ref[3, source_slot(j, ghost, row == 0, split, 1)])


def pack(split, row, faces, pos, feat, rows):
    ghost = faces.shape[1]
    depth = feat.shape[0] + 8
    vm = pl.BlockSpec(memory_space=pltpu.VMEM)
    sm = pl.BlockSpec(memory_space=pltpu.SMEM)
    face = jax.ShapeDtypeStruct((ghost, depth, LANES), f32)
    slot = jax.ShapeDtypeStruct((depth, LANES), f32)
    outs = pl.pallas_call(
        functools.partial(pack_kernel, rows),
        out_shape=(face, face) + (slot,) * (2 * ghost),
        in_specs=[sm, sm, sm, vm, vm],
        out_specs=(vm,) * (2 + 2 * ghost),
        name="pack",
    )(split, row, faces, pos, feat)
    return outs[0], outs[1], outs[2:]


def row_permutation(rows, cols, upward, shift):
    pairs = []
    for g in range(rows):
        for c in range(cols):
            if upward:
                target = (g + 1, c) if g < rows - 1 else (0, (c + shift) % cols)
            else:
                target = (g - 1, c) if g > 0 else (rows - 1, (c - shift) % cols)
            pairs.append((c * rows + g, target[1] * rows + target[0]))
    return pairs


def slot_permutations(rows, cols, ghost, shift, split):
    perms = [row_permutation(rows, cols, True, shift + (1 if j < split else 0)) for j in range(ghost)]
    perms += [row_permutation(rows, cols, False, shift + (1 if j >= ghost - split else 0)) for j in range(ghost)]
    return perms


def crossing(slots, branch, rows, cols, ghost, back):
    def case(number):
        shift, split = divmod(number, ghost)
        perms = slot_permutations(rows, cols, ghost, shift, split)

        def route(values):
            outs = []
            for value, perm in zip(values, perms):
                pairs = [(b, a) for a, b in perm] if back else perm
                outs.append(lax.ppermute(value, ("flow", "grad"), pairs))
            return tuple(outs)

        return route

    return lax.switch(branch, [case(number) for number in range(cols * ghost)], tuple(slots))


def ring(value, by):
    peers = lax.axis_size("flow")
    return lax.ppermute(value, "flow", [(i, (i + by) % peers) for i in range(peers)])


def body(
    positions,
    features,
    neighbours,
    face_blocks,
    shear_cells,
    split_block,
    radial_in,
    radial_out,
    mixing,
    readout,
):
    own_pos = positions[:, 0, :]
    own_feat = features[0]
    faces = face_blocks[0]
    entries, atoms = neighbours.shape[1:]
    ghost = faces.shape[1]
    rows = lax.axis_size("grad")
    cols = lax.axis_size("flow")
    row = lax.axis_index("grad")
    row_array = row.astype(jnp.int32).reshape(1)
    split = split_block[0]
    whole = split // ghost
    branch = lax.rem(shear_cells[0] + whole, cols) * ghost + (split - whole * ghost)
    tile = GROUPS * entries
    idx = jnp.transpose(neighbours[0]).reshape(atoms // GROUPS, tile)

    left, right, slots = pack(split_block, row_array, faces, own_pos, own_feat, rows)
    left = ring(left, 1)
    right = ring(right, -1)
    slots = crossing(slots, branch, rows, cols, ghost, False)
    energy, own, ghosts = core(
        split_block, row_array, idx, own_pos, own_feat, radial_in, radial_out, mixing,
        readout.reshape(1, -1), left, right, slots, rows,
    )
    back_left = ring(ghosts[0], -1)
    back_right = ring(ghosts[1], 1)
    back = [ghosts[2, j] for j in range(ghost)] + [ghosts[3, j] for j in range(ghost)]
    back = crossing(back, branch, rows, cols, ghost, True)
    returned = [(faces[0, j], back_left[j]) for j in range(ghost)]
    returned += [(faces[1, j], back_right[j]) for j in range(ghost)]
    for j in range(ghost):
        returned.append((faces[2, source_slot(j, ghost, row == rows - 1, split, -1)], back[j]))
    for j in range(ghost):
        returned.append((faces[3, source_slot(j, ghost, row == 0, split, 1)], back[ghost + j]))
    blocks = []
    for number in range(atoms // LANES):
        total = own[:, number * LANES : (number + 1) * LANES]
        for block, value in returned:
            total = total + jnp.where(block == number, value, 0.0)
        blocks.append(-total)
    forces = jnp.concatenate(blocks, axis=1)
    return (energy, forces.reshape(3, 1, atoms))


def solution(mesh):
    in_specs = (
        P(None, "grad", "flow"),
        P("grad", None, "flow"),
        P("grad", None, "flow"),
        P("grad", None, "flow"),
        P(),
        P(),
        P(),
        P(),
        P(),
        P(),
    )
    out_specs = (P("grad", "flow"), P(None, "grad", "flow"))
    return jax.shard_map(body, mesh=mesh, in_specs=in_specs, out_specs=out_specs, check_vma=False)
```

time: 235 us -> 86 us (0.37)
  matrix products: 113 us -> 0 us
  local copies, waits for them, and re-layouts: 47.4 us -> 4.73 us
  Pallas kernels: 0 us -> 37 us
  waiting for transfers between devices: 26.1 us -> 11.2 us
  other arithmetic: 13.5 us -> 1.43 us
  between operations: 2.48 us -> 12.2 us
  starting transfers between devices: 27.6 us -> 18.2 us
  loops' own time: 4.22 us -> 0.04 us
    dot_general x102 -> x0, matrix products: 113 us -> none  [the longest x24 39.5 us: contribution(): return jnp.einsum('gbc,mgb->mcb', weighted, harmonic, precision=highest)]
    pallas_call x0 -> x2, Pallas kernels: none -> 37 us  [the longest x1 35.4 us: core(): pl.pallas_call(functools.partial(core_kernel, groups, neighbours, number,...]
    gather x8 -> x0, local copies, waits for them, and re-layouts: 22.5 us -> none  [forward(): jnp.take(feat_rows, group_idx.reshape(-1), axis=0)]
    ppermute x24 -> x12, waiting for transfers between devices: 26.1 us -> 11.2 us  [the longest x8 9.47 us: route(): outs.append(lax.ppermute(value, ('flow', 'grad'), pairs))]
    ppermute x24 -> x12, starting transfers between devices: 27.6 us -> 18.2 us  [the longest x8 13.2 us: route(): outs.append(lax.ppermute(value, ('flow', 'grad'), pairs))]
    while x56 -> x0, local copies, waits for them, and re-layouts: 8.9 us -> none
    dynamic_update_slice x10 -> x0, other arithmetic: 8.06 us -> none  [the longest x8 8.03 us: block_pass(): lax.scan(forward, starting, chosen_groups)]
    another operation x5 -> x2, loops' own time: 4.22 us -> 0.04 us  [crossing(): lax.switch(branch, [case(number) for number in range(cols * ghost)], tupl...]
  transfers between devices with their start and end apart: 24 -> 12, of which waited for: 13 -> 7; matrix products, arithmetic and copies ran while one was open for 4% -> 2% of each run, Pallas kernels for 0% -> 0%
where the time goes in v1:
time: 86 us; the launch traced here: 84.9 us
  Pallas kernels  37 us (43%)
  starting transfers between devices  18.2 us (21%)
  between operations  12.2 us (14%)
  waiting for transfers between devices  11.2 us (13%)
  local copies, waits for them, and re-layouts  4.73 us (6%)
  other arithmetic  1.43 us (2%)
    pallas_call x1, Pallas kernels, core(): pl.pallas_call(functools.partial(core_kernel, groups, neighbours, number,...  35.4 us
    ppermute x8, starting transfers between devices, route(): outs.append(lax.ppermute(value, ('flow', 'grad'), pairs))  13.2 us
    ppermute x8, waiting for transfers between devices, route(): outs.append(lax.ppermute(value, ('flow', 'grad'), pairs))  9.47 us
    ppermute x4, starting transfers between devices, ring(): lax.ppermute(value, 'flow', [(i, (i + by) % peers) for i in range(peers)])  5.06 us
    unnamed x22, local copies, waits for them, and re-layouts  2.56 us
  transfers between devices with their start and end apart: 12, of which 7 were waited for; matrix products, arithmetic and copies ran while one was open for 2% of the time, Pallas kernels for 0%

profile of v1, /device:TPU:0, one launch (start us, length us, event | category | flops | bytes accessed | tf_op | source)
XLA Modules:
  0.0 84.9 jit_solution(16586375240037454654)
XLA Ops:
  0.6 0.0 copy-start.8
  1.3 0.0 copy-done.8
  1.3 0.6 copy.20
  1.9 0.7 copy-done.7
  2.6 0.7 copy.16.faces_ref
  3.2 1.7 %pack.1 = (f32[2,136,128]{2,1,0:T(8,128)}, f32[2,136,128]{2,1,0:T(8,128)}, f32[136,128]{1,0:T(8,128)S(1)}, f32[136,128]{1,0:T(8,128)S(1)}, f32[136,128]{1,0:T(8,128)S(1)}, /*index=5*/f32[136,128]{1,0:T(8,128)S(1)}) custom-call(s32[1]{0:T(128)} %copy.150.split_ref, s32[1]{0:T(128)} %bitcast.row_ref, s32[4,2]{1,0:T(4,128)} %copy.16.faces_ref, ...), custom_call_target="tpu_custom_call" | custom-call | tf_op jit(solution)/shard_map/pack/pallas_call | solution.py:337
  4.9 0.5 collective-permute-start.128
  6.1 0.0 copy-start.6
  6.1 12.3 %conditional.2 = (f32[136,128]{1,0:T(8,128)}, f32[136,128]{1,0:T(8,128)}, f32[136,128]{1,0:T(8,128)}, f32[136,128]{1,0:T(8,128)}) conditional(s32[]{:T(128)} %clamp.4, (f32[136,128]{1,0:T(8,128)S(1)}, f32[136,128]{1,0:T(8,128)S(1)}, f32[136,128]{1,0:T(8,128)S(1)}, f32[136,128]{1,0:T(8,128)S(1)}) %tuple.136, ...), branch_computations={%region_0.1_spmd, %region_1.2_spmd, %region_2.3_spmd, %region_3.4_... | conditional | bytes 1114304 | solution.py:379
  6.1 2.7 %collective-permute-start.60 = (f32[136,128]{1,0:T(8,128)S(1)}, f32[136,128]{1,0:T(8,128)}, u32[]{:S(2)}, u32[]{:S(2)}) collective-permute-start(f32[136,128]{1,0:T(8,128)S(1)} %get-tuple-element.316), channel_id=1, source_target_pairs={{0,1},{4,5},{8,9},{12,13},{16,17},{20,21},{24,25},{28,29},{1,2},{5... | collective-permute-start | bytes 208904 | tf_op jit(solution)/shard_map/cond/branch_15_fun/ppermute | solution.py:374
  8.8 1.6 %collective-permute-start.61 = (f32[136,128]{1,0:T(8,128)S(1)}, f32[136,128]{1,0:T(8,128)}, u32[]{:S(2)}, u32[]{:S(2)}) collective-permute-start(f32[136,128]{1,0:T(8,128)S(1)} %get-tuple-element.317), channel_id=1, source_target_pairs={{0,1},{4,5},{8,9},{12,13},{16,17},{20,21},{24,25},{28,29},{1,2},{5... | collective-permute-start | bytes 208904 | tf_op jit(solution)/shard_map/cond/branch_15_fun/ppermute | solution.py:374
  10.3 2.0 %collective-permute-start.62 = (f32[136,128]{1,0:T(8,128)S(1)}, f32[136,128]{1,0:T(8,128)}, u32[]{:S(2)}, u32[]{:S(2)}) collective-permute-start(f32[136,128]{1,0:T(8,128)S(1)} %get-tuple-element.318), channel_id=1, source_target_pairs={{0,7},{4,11},{8,15},{12,19},{16,23},{20,27},{24,31},{28,3},{1,0},{... | collective-permute-start | bytes 208904 | tf_op jit(solution)/shard_map/cond/branch_15_fun/ppermute | solution.py:374
  12.3 2.0 %collective-permute-start.63 = (f32[136,128]{1,0:T(8,128)S(1)}, f32[136,128]{1,0:T(8,128)}, u32[]{:S(2)}, u32[]{:S(2)}) collective-permute-start(f32[136,128]{1,0:T(8,128)S(1)} %get-tuple-element.319), channel_id=1, source_target_pairs={{0,3},{4,7},{8,11},{12,15},{16,19},{20,23},{24,27},{28,31},{1,0},{... | collective-permute-start | bytes 208904 | tf_op jit(solution)/shard_map/cond/branch_15_fun/ppermute | solution.py:374
  14.3 0.0 collective-permute-done.60
  14.4 0.5 collective-permute-done.61
  14.9 1.9 %collective-permute-done.62 = f32[136,128]{1,0:T(8,128)} collective-permute-done((f32[136,128]{1,0:T(8,128)S(1)}, f32[136,128]{1,0:T(8,128)}, u32[]{:S(2)}, u32[]{:S(2)}) %collective-permute-start.62) | collective-permute-done | bytes 69664 | tf_op jit(solution)/shard_map/cond/branch_15_fun/ppermute | solution.py:374
  16.8 1.5 %collective-permute-done.63 = f32[136,128]{1,0:T(8,128)} collective-permute-done((f32[136,128]{1,0:T(8,128)S(1)}, f32[136,128]{1,0:T(8,128)}, u32[]{:S(2)}, u32[]{:S(2)}) %collective-permute-start.63) | collective-permute-done | bytes 69664 | tf_op jit(solution)/shard_map/cond/branch_15_fun/ppermute | solution.py:374
  18.4 0.0 copy-done.9
  18.4 1.8 %collective-permute-start.129 = (f32[2,136,128]{2,1,0:T(8,128)S(1)}, f32[2,136,128]{2,1,0:T(8,128)S(1)}, u32[]{:S(2)}, u32[]{:S(2)}) collective-permute-start(f32[2,136,128]{2,1,0:T(8,128)S(1)} %copy-done.9), channel_id=1, source_target_pairs={{0,28},{4,0},{8,4},{12,8},{16,12},{20,16},{24,20},{28,24},{1,29},{... | collective-permute-start | bytes 417800 | tf_op jit(solution)/shard_map/ppermute | solution.py:384
  20.1 0.0 copy-done.6
  20.1 0.1 copy.15
  20.2 0.0 copy-start
  20.3 0.0 copy-start.3
  20.3 0.1 reshape.81.idx_ref
  20.4 0.7 fusion.10
  21.0 0.0 collective-permute-done.128.left_ref
  21.0 1.7 %collective-permute-done.129.right_ref = f32[2,136,128]{2,1,0:T(8,128)S(1)} collective-permute-done((f32[2,136,128]{2,1,0:T(8,128)S(1)}, f32[2,136,128]{2,1,0:T(8,128)S(1)}, u32[]{:S(2)}, u32[]{:S(2)}) %collective-permute-start.129) | collective-permute-done | bytes 139296 | tf_op jit(solution)/shard_map/ppermute | solution.py:384
  22.8 0.0 copy-done.1
  22.8 0.7 copy-done.4
  23.4 0.0 copy-done.2
  23.4 35.4 %core.1 = (f32[1,256]{1,0:T(1,128)}, f32[3,256]{1,0:T(4,128)S(1)}, f32[4,2,3,128]{3,2,1,0:T(4,128)S(1)}) custom-call(s32[1]{0:T(128)} %copy.150.split_ref, s32[1]{0:T(128)} %bitcast.row_ref, s32[32,256]{1,0:T(8,128)S(1)} %reshape.81.idx_ref, f32[3,256]{1,0:T(4,128)S(1)} %bitcast.102, f32[128,256]{1,0:T(8,128)S(1)} %bitcast.100, f32[8,64]{1,0:T(8,128)S(1)} %copy-done.4, ...), custom_call_target="tpu_custom_call" | custom-call | tf_op jit(solution)/shard_map/core/pallas_call | solution.py:282
  58.8 2.8 %collective-permute-start.130 = (f32[2,3,128]{2,1,0:T(4,128)S(1)}, f32[2,3,128]{2,1,0:T(4,128)S(1)}, u32[]{:S(2)}, u32[]{:S(2)}) collective-permute-start(f32[2,3,128]{2,1,0:T(4,128)S(1)} %get-tuple-element.424), channel_id=1, source_target_pairs={{0,28},{4,0},{8,4},{12,8},{16,12},{20,16},{24,20},{28,24},{1,29},{... | collective-permute-start | bytes 9224 | tf_op jit(solution)/shard_map/ppermute | solution.py:384
  61.6 10.4 %conditional.3 = (f32[3,128]{1,0:T(4,128)}, f32[3,128]{1,0:T(4,128)}, f32[3,128]{1,0:T(4,128)}, f32[3,128]{1,0:T(4,128)}) conditional(s32[]{:T(128)} %clamp.4, (f32[3,128]{1,0:T(4,128)S(1)}, f32[3,128]{1,0:T(4,128)S(1)}, f32[3,128]{1,0:T(4,128)S(1)}, f32[3,128]{1,0:T(4,128)S(1)}) %tuple.137, (f32[3,128]{1,0:T(4,128)S(1)}, ...), branch_computations={%region_16.17_spmd, %region_17.18_spmd, %region_18.19_spmd, %regio... | conditional | bytes 24768 | solution.py:379
  61.6 2.9 %collective-permute-start.124 = (f32[3,128]{1,0:T(4,128)S(1)}, f32[3,128]{1,0:T(4,128)}, u32[]{:S(2)}, u32[]{:S(2)}) collective-permute-start(f32[3,128]{1,0:T(4,128)S(1)} %get-tuple-element.380), channel_id=1, source_target_pairs={{1,0},{5,4},{9,8},{13,12},{17,16},{21,20},{25,24},{29,28},{2,1},{6... | collective-permute-start | bytes 4616 | tf_op jit(solution)/shard_map/cond/branch_15_fun/ppermute | solution.py:374
  64.5 0.0 collective-permute-start.125
  64.5 2.0 %collective-permute-start.126 = (f32[3,128]{1,0:T(4,128)S(1)}, f32[3,128]{1,0:T(4,128)}, u32[]{:S(2)}, u32[]{:S(2)}) collective-permute-start(f32[3,128]{1,0:T(4,128)S(1)} %get-tuple-element.382), channel_id=1, source_target_pairs={{7,0},{11,4},{15,8},{19,12},{23,16},{27,20},{31,24},{3,28},{0,1},{... | collective-permute-start | bytes 4616 | tf_op jit(solution)/shard_map/cond/branch_15_fun/ppermute | solution.py:374
  66.5 0.0 collective-permute-start.127
  66.5 0.0 collective-permute-done.124
  66.5 1.6 %collective-permute-done.125 = f32[3,128]{1,0:T(4,128)} collective-permute-done((f32[3,128]{1,0:T(4,128)S(1)}, f32[3,128]{1,0:T(4,128)}, u32[]{:S(2)}, u32[]{:S(2)}) %collective-permute-start.125) | collective-permute-done | bytes 1568 | tf_op jit(solution)/shard_map/cond/branch_15_fun/ppermute | solution.py:374
  68.2 1.2 %collective-permute-done.126 = f32[3,128]{1,0:T(4,128)} collective-permute-done((f32[3,128]{1,0:T(4,128)S(1)}, f32[3,128]{1,0:T(4,128)}, u32[]{:S(2)}, u32[]{:S(2)}) %collective-permute-start.126) | collective-permute-done | bytes 1568 | tf_op jit(solution)/shard_map/cond/branch_15_fun/ppermute | solution.py:374
  69.4 2.6 %collective-permute-done.127 = f32[3,128]{1,0:T(4,128)} collective-permute-done((f32[3,128]{1,0:T(4,128)S(1)}, f32[3,128]{1,0:T(4,128)}, u32[]{:S(2)}, u32[]{:S(2)}) %collective-permute-start.127) | collective-permute-done | bytes 1568 | tf_op jit(solution)/shard_map/cond/branch_15_fun/ppermute | solution.py:374
  72.0 0.0 collective-permute-start.131
  72.0 0.7 constant_dynamic-slice_fusion.3
  82.8 0.0 collective-permute-done.130
  82.8 0.0 collective-permute-done.131
  82.8 0.7 fusion.9
  83.6 0.7 fusion.4
  84.3 0.6 copy.17
  (12 shorter events, 0.0 us)
Async XLA Ops:
  0.6 0.7 copy-start.8
  1.9 0.7 copy-start.7
  4.9 13.5 %copy-start.9 = (f32[2,136,128]{2,1,0:T(8,128)S(1)}, f32[2,136,128]{2,1,0:T(8,128)}, u32[]{:S(2)}) copy-start(f32[2,136,128]{2,1,0:T(8,128)} %get-tuple-element.404) | copy-start | bytes 417796
  4.9 16.1 %collective-permute-start.128 = (f32[2,136,128]{2,1,0:T(8,128)}, f32[2,136,128]{2,1,0:T(8,128)S(1)}, u32[]{:S(2)}, u32[]{:S(2)}) collective-permute-start(f32[2,136,128]{2,1,0:T(8,128)} %get-tuple-element.403), channel_id=1, source_target_pairs={{0,4},{4,8},{8,12},{12,16},{16,20},{20,24},{24,28},{28,0},{1,5},{5... | collective-permute-start | bytes 417800 | tf_op jit(solution)/shard_map/ppermute | solution.py:384
  6.1 14.1 %copy-start.6 = (s32[1,32,256]{2,1,0:T(8,128)S(1)}, s32[1,32,256]{2,1,0:T(8,128)}, u32[]{:S(2)}) copy-start(s32[1,32,256]{2,1,0:T(8,128)} %param.44) | copy-start | bytes 98308
  6.1 8.2 %collective-permute-start.60 = (f32[136,128]{1,0:T(8,128)S(1)}, f32[136,128]{1,0:T(8,128)}, u32[]{:S(2)}, u32[]{:S(2)}) collective-permute-start(f32[136,128]{1,0:T(8,128)S(1)} %get-tuple-element.316), channel_id=1, source_target_pairs={{0,1},{4,5},{8,9},{12,13},{16,17},{20,21},{24,25},{28,29},{1,2},{5... | collective-permute-start | bytes 208904 | tf_op jit(solution)/shard_map/cond/branch_15_fun/ppermute | solution.py:374
  8.8 6.1 %collective-permute-start.61 = (f32[136,128]{1,0:T(8,128)S(1)}, f32[136,128]{1,0:T(8,128)}, u32[]{:S(2)}, u32[]{:S(2)}) collective-permute-start(f32[136,128]{1,0:T(8,128)S(1)} %get-tuple-element.317), channel_id=1, source_target_pairs={{0,1},{4,5},{8,9},{12,13},{16,17},{20,21},{24,25},{28,29},{1,2},{5... | collective-permute-start | bytes 208904 | tf_op jit(solution)/shard_map/cond/branch_15_fun/ppermute | solution.py:374
  10.3 6.5 %collective-permute-start.62 = (f32[136,128]{1,0:T(8,128)S(1)}, f32[136,128]{1,0:T(8,128)}, u32[]{:S(2)}, u32[]{:S(2)}) collective-permute-start(f32[136,128]{1,0:T(8,128)S(1)} %get-tuple-element.318), channel_id=1, source_target_pairs={{0,7},{4,11},{8,15},{12,19},{16,23},{20,27},{24,31},{28,3},{1,0},{... | collective-permute-start | bytes 208904 | tf_op jit(solution)/shard_map/cond/branch_15_fun/ppermute | solution.py:374
  12.3 6.1 %collective-permute-start.63 = (f32[136,128]{1,0:T(8,128)S(1)}, f32[136,128]{1,0:T(8,128)}, u32[]{:S(2)}, u32[]{:S(2)}) collective-permute-start(f32[136,128]{1,0:T(8,128)S(1)} %get-tuple-element.319), channel_id=1, source_target_pairs={{0,3},{4,7},{8,11},{12,15},{16,19},{20,23},{24,27},{28,31},{1,0},{... | collective-permute-start | bytes 208904 | tf_op jit(solution)/shard_map/cond/branch_15_fun/ppermute | solution.py:374
  18.4 4.4 %copy-start.1 = (f32[3,128,128]{2,1,0:T(8,128)S(1)}, f32[3,128,128]{2,1,0:T(8,128)}, u32[]{:S(2)}) copy-start(f32[3,128,128]{2,1,0:T(8,128)} %mix_ref.1) | copy-start | bytes 589828
  18.4 4.4 %collective-permute-start.129 = (f32[2,136,128]{2,1,0:T(8,128)S(1)}, f32[2,136,128]{2,1,0:T(8,128)S(1)}, u32[]{:S(2)}, u32[]{:S(2)}) collective-permute-start(f32[2,136,128]{2,1,0:T(8,128)S(1)} %copy-done.9), channel_id=1, source_target_pairs={{0,28},{4,0},{8,4},{12,8},{16,12},{20,16},{24,20},{28,24},{1,29},{... | collective-permute-start | bytes 417800 | tf_op jit(solution)/shard_map/ppermute | solution.py:384
  20.2 2.5 %copy-start = (f32[1,128,256]{2,1,0:T(8,128)S(1)}, f32[1,128,256]{2,1,0:T(8,128)}, u32[]{:S(2)}) copy-start(f32[1,128,256]{2,1,0:T(8,128)} %param.43) | copy-start | bytes 393220
  20.3 2.5 %copy-start.3 = (f32[64,128]{1,0:T(8,128)S(1)}, f32[64,128]{1,0:T(8,128)}, u32[]{:S(2)}) copy-start(f32[64,128]{1,0:T(8,128)} %wout_ref.1) | copy-start | bytes 98308
  22.7 0.7 copy-start.4
  22.7 0.7 copy-start.2
  22.7 0.7 copy-start.5
  58.8 24.0 %collective-permute-start.130 = (f32[2,3,128]{2,1,0:T(4,128)S(1)}, f32[2,3,128]{2,1,0:T(4,128)S(1)}, u32[]{:S(2)}, u32[]{:S(2)}) collective-permute-start(f32[2,3,128]{2,1,0:T(4,128)S(1)} %get-tuple-element.424), channel_id=1, source_target_pairs={{0,28},{4,0},{8,4},{12,8},{16,12},{20,16},{24,20},{28,24},{1,29},{... | collective-permute-start | bytes 9224 | tf_op jit(solution)/shard_map/ppermute | solution.py:384
  61.6 4.9 %collective-permute-start.124 = (f32[3,128]{1,0:T(4,128)S(1)}, f32[3,128]{1,0:T(4,128)}, u32[]{:S(2)}, u32[]{:S(2)}) collective-permute-start(f32[3,128]{1,0:T(4,128)S(1)} %get-tuple-element.380), channel_id=1, source_target_pairs={{1,0},{5,4},{9,8},{13,12},{17,16},{21,20},{25,24},{29,28},{2,1},{6... | collective-permute-start | bytes 4616 | tf_op jit(solution)/shard_map/cond/branch_15_fun/ppermute | solution.py:374
  64.5 3.7 %collective-permute-start.125 = (f32[3,128]{1,0:T(4,128)S(1)}, f32[3,128]{1,0:T(4,128)}, u32[]{:S(2)}, u32[]{:S(2)}) collective-permute-start(f32[3,128]{1,0:T(4,128)S(1)} %get-tuple-element.381), channel_id=1, source_target_pairs={{1,0},{5,4},{9,8},{13,12},{17,16},{21,20},{25,24},{29,28},{2,1},{6... | collective-permute-start | bytes 4616 | tf_op jit(solution)/shard_map/cond/branch_15_fun/ppermute | solution.py:374
  64.5 4.9 %collective-permute-start.126 = (f32[3,128]{1,0:T(4,128)S(1)}, f32[3,128]{1,0:T(4,128)}, u32[]{:S(2)}, u32[]{:S(2)}) collective-permute-start(f32[3,128]{1,0:T(4,128)S(1)} %get-tuple-element.382), channel_id=1, source_target_pairs={{7,0},{11,4},{15,8},{19,12},{23,16},{27,20},{31,24},{3,28},{0,1},{... | collective-permute-start | bytes 4616 | tf_op jit(solution)/shard_map/cond/branch_15_fun/ppermute | solution.py:374
  66.5 5.5 %collective-permute-start.127 = (f32[3,128]{1,0:T(4,128)S(1)}, f32[3,128]{1,0:T(4,128)}, u32[]{:S(2)}, u32[]{:S(2)}) collective-permute-start(f32[3,128]{1,0:T(4,128)S(1)} %get-tuple-element.383), channel_id=1, source_target_pairs={{3,0},{7,4},{11,8},{15,12},{19,16},{23,20},{27,24},{31,28},{0,1},{... | collective-permute-start | bytes 4616 | tf_op jit(solution)/shard_map/cond/branch_15_fun/ppermute | solution.py:374
  72.0 10.8 %collective-permute-start.131 = (f32[2,3,128]{2,1,0:T(4,128)S(1)}, f32[2,3,128]{2,1,0:T(4,128)S(1)}, u32[]{:S(2)}, u32[]{:S(2)}) collective-permute-start(f32[2,3,128]{2,1,0:T(4,128)S(1)} %get-tuple-element.425), channel_id=1, source_target_pairs={{0,4},{4,8},{8,12},{12,16},{16,20},{20,24},{24,28},{28,0},{1,5},{5... | collective-permute-start | bytes 9224 | tf_op jit(solution)/shard_map/ppermute | solution.py:384
